TPU v7x, 32 devices: a whole 2x2x4 slice. The times are simulated.
32 devices in a mesh: loop: 8 (over z, x), rep: 4 (over y, core).
Axes of the slice: x: 2, y: 2, z: 4, core: 2. Of those that a mesh axis runs over, the one named last changes fastest.
Arguments:
- features: float32 [4096, 128], P('loop'), may hold values from -6 to 6
- weight: float32 [128, 256], replicated, may hold values from -0.5 to 0.5
- bias: float32 [256], replicated, may hold values from -3 to 3
- tile_values: float32 [512, 128, 128], P(('loop', 'rep')), may hold values from -0.125 to 0.125
- tile_rows: int32 [512], P(('loop', 'rep')), may hold values from 0 to 31, as said below
- tile_cols: int32 [512], P(('loop', 'rep')), may hold values from 0 to 31, as said below
- tile_count: int32 [32], P(('loop', 'rep')), may hold values from 1 to 16, as said below
- cotangent: float32 [4096, 256], P('loop'), may hold values from -0.6 to 0.6
Outputs:
- output: float32 [4096, 256], P('loop')
- grad_features: float32 [4096, 128], P('loop')
- grad_weight: float32 [128, 256], replicated
- grad_bias: float32 [256], replicated
Inputs may be any that keep to these rules, and one draw needn't show every extreme that they name: `tile_rows`: every slot of a device at loop index l names a row block from l * 4 to (l + 1) * 4 - 1. `tile_cols`: for every loop index m, the live slots of one device name at most 2 different column blocks from m * 4 to (m + 1) * 4 - 1; for every loop index some device names exactly 2 of one such range. `tile_count`: for every loop index some device has all 16 slots live.
All inputs are finite; a program needn't handle non-finite values.
Results may differ from a plain program's by a relative error of at most 0.0001.
Values sent between devices are 32-bit elements; how exact they have to be, the bound alone decides.
No kernel may reach another device: no remote copies, remote signals or barrier semaphores. Data moves between devices by JAX's collectives and lax.ppermute only.
A program may use at most 64 MiB of HBM per device.

v0:
```python
import jax
import jax.numpy as jnp
from jax import lax
from jax.sharding import PartitionSpec as P


def per_device(features, weight, bias, tile_values, tile_rows, tile_cols, tile_count, cotangent):
    highest = lax.Precision.HIGHEST
    tile_side = tile_values.shape[1]
    rows_here = features.shape[0]
    nblocks = rows_here // tile_side
    slots = tile_values.shape[0]
    local_rows = tile_rows - lax.axis_index("loop") * nblocks
    live_slot = (jnp.arange(slots, dtype=jnp.int32) < tile_count[0]).astype(jnp.float32)
    row_pick = (local_rows[:, None] == jnp.arange(nblocks, dtype=jnp.int32)[None, :]).astype(
        jnp.float32
    )
    row_pick = row_pick * live_slot[:, None]
    gathered = lax.all_gather(features, "loop", axis=0, tiled=True)
    width = gathered.shape[1]
    blocks = gathered.reshape(-1, tile_side, width)[tile_cols]
    products = jnp.einsum("kij,kjf->kif", tile_values, blocks, precision=highest)
    aggregated = lax.psum(
        jnp.einsum("kb,kif->bif", row_pick, products, precision=highest), "rep"
    ).reshape(rows_here, -1)
    preactive = jnp.dot(aggregated, weight, precision=highest) + bias
    logistic = jax.nn.sigmoid(preactive)
    output = preactive * logistic
    gradient = cotangent * logistic * (1.0 + preactive * (1.0 - logistic))
    spread = jnp.dot(gradient, weight.T, precision=highest)
    source_blocks = spread.reshape(nblocks, tile_side, spread.shape[1])[
        jnp.clip(local_rows, 0, nblocks - 1)
    ]
    outgoing = jnp.einsum("kji,kjf->kif", tile_values, source_blocks, precision=highest)
    outgoing = outgoing * live_slot[:, None, None]
    span = rows_here * lax.axis_size("loop") // tile_side + 2
    column_pick = (tile_cols[:, None] == jnp.arange(span, dtype=jnp.int32)[None, :]).astype(
        jnp.float32
    )
    placed = jnp.einsum("kb,kif->bif", column_pick, outgoing, precision=highest)
    placed = placed.reshape(span * tile_side, outgoing.shape[2])
    term = lax.psum_scatter(
        lax.slice_in_dim(placed, 0, rows_here * lax.axis_size("loop"), axis=0),
        "loop",
        scatter_dimension=0,
        tiled=True,
    )
    own_rows = lax.psum(term, "rep")
    weight_term = jnp.dot(aggregated.T, gradient, precision=highest)
    bias_term = jnp.sum(gradient, axis=0)
    grad_weight, grad_bias = lax.psum((weight_term, bias_term), "loop")
    return (output, own_rows, grad_weight, grad_bias)


def solution(mesh):
    return jax.shard_map(
        per_device,
        mesh=mesh,
        in_specs=(
            P("loop", None),
            P(),
            P(),
            P(("loop", "rep"), None, None),
            P(("loop", "rep")),
            P(("loop", "rep")),
            P(("loop", "rep")),
            P("loop", None),
        ),
        out_specs=(P("loop", None), P("loop", None), P(), P()),
        check_vma=False,
    )
```

profile of v0, /device:TPU:0, one launch (start us, length us, event | category | flops | bytes accessed | tf_op | source)
XLA Modules:
  0.0 293.9 jit_solution(1856292996977088046)
XLA Ops:
  7.2 0.7 all-gather.2.cloned.1.call-update
  8.6 0.7 compare_select_fusion.1
  9.3 0.7 compare_select_fusion
  10.0 52.0 %all-gather.2.cloned.1.call-done = f32[4096,128]{1,0:T(8,128)} async-done(((f32[512,128]{1,0:T(8,128)}), f32[4096,128]{1,0:T(8,128)}) %all-gather.2.cloned.1.call-update) | async-done | bytes 2097168 | tf_op jit(solution)/shard_map/all_gather | solution.py:19
  62.0 2.2 gather_fusion
  64.2 1.8 fusion.16
  66.1 0.5 copy.14
  66.6 0.6 fusion.2
  67.2 0.7 copy.12
  68.1 30.8 %all-reduce.4.cloned.1.call-done = f32[512,128]{1,0:T(8,128)} async-done(((f32[512,128]{1,0:T(8,128)}), f32[512,128]{1,0:T(8,128)}) %all-reduce.4.cloned.1.call-update) | async-done | bytes 262160 | tf_op jit(solution)/shard_map/psum | solution.py:23
  98.9 2.5 fusion.15
  101.4 0.6 fusion.17
  102.2 0.6 gather_fusion.1
  102.8 1.8 fusion.18
  105.2 1.0 fusion
  106.2 2.6 copy.13
  108.9 1.0 copy-done.2
  109.9 1.3 fusion.19
  111.3 66.0 %reduce-scatter.2.cloned.1.call-done = f32[512,128]{1,0:T(8,128)} async-done(((f32[4096,128]{1,0:T(8,128)}), f32[512,128]{1,0:T(8,128)}) %reduce-scatter.2.cloned.1.call-update) | async-done | bytes 262160 | tf_op jit(solution)/shard_map/reduce_scatter | solution.py:42
  177.3 19.7 %psum.31 = f32[256]{0:T(256)} all-reduce(f32[256]{0:T(256)S(1)} %get-tuple-element.4), channel_id=1, replica_groups=mesh['loop'=8,'rep'=4] {'loop'}, use_global_device_ids=true, to_apply=%region_5.6 | all-reduce | flops 256 | bytes 2048 | tf_op jit(solution)/shard_map/psum | solution.py:51
  197.0 53.6 %all-reduce.8.cloned.1.call-done = f32[128,256]{1,0:T(8,128)} async-done(((f32[128,256]{1,0:T(8,128)}), f32[128,256]{1,0:T(8,128)}) %all-reduce.8.cloned.1.call-update) | async-done | bytes 131088 | tf_op jit(solution)/shard_map/psum | solution.py:51
  250.6 33.6 %all-reduce.6.cloned.1.call-done = f32[512,128]{1,0:T(8,128)} async-done(((f32[512,128]{1,0:T(8,128)}), f32[512,128]{1,0:T(8,128)}) %all-reduce.6.cloned.1.call-update) | async-done | bytes 262160 | tf_op jit(solution)/shard_map/psum | solution.py:48
  284.2 1.7 copy.20
  285.8 1.6 copy.21
  (29 shorter events, 1.2 us)
Async XLA Ops:
  7.2 57.0 %copy-start = (f32[16,128,128]{2,1,0:T(8,128)S(1)}, f32[16,128,128]{2,1,0:T(8,128)}, u32[]{:S(2)}) copy-start(f32[16,128,128]{2,1,0:T(8,128)} %param.11) | copy-start | bytes 3145732
  7.2 54.8 %all-gather.2.cloned.1.call-start = ((), (), s32[]{:S(2)}) async-start(), calls=%async_computation.1 | async-start | bytes 2359296 | tf_op jit(solution)/shard_map/all_gather | solution.py:19
  7.9 91.0 %all-reduce.4.cloned.1.call-start = ((), (), s32[]{:S(2)}) async-start(), calls=%async_computation.2 | async-start | bytes 524288 | tf_op jit(solution)/shard_map/psum | solution.py:23
  66.0 2.0 copy-start.5
  66.0 32.9 %copy-start.4 = (f32[128,256]{1,0:T(8,128)S(1)}, f32[128,256]{1,0:T(8,128)}, u32[]{:S(2)}) copy-start(f32[128,256]{1,0:T(8,128)} %param.9) | copy-start | bytes 393220
  66.0 32.9 %copy-start.7 = (f32[256]{0:T(256)S(1)}, f32[256]{0:T(256)}, u32[]{:S(2)}) copy-start(f32[256]{0:T(256)} %param.10) | copy-start | bytes 3076
  66.6 32.4 %copy-start.6 = (f32[512,256]{1,0:T(8,128)S(1)}, f32[512,256]{1,0:T(8,128)}, u32[]{:S(2)}) copy-start(f32[512,256]{1,0:T(8,128)} %param.15) | copy-start | bytes 1572868
  68.0 109.3 %reduce-scatter.2.cloned.1.call-start = ((), (), s32[]{:S(2)}) async-start(), calls=%async_computation.3 | async-start | bytes 2359296 | tf_op jit(solution)/shard_map/reduce_scatter | solution.py:42
  101.4 0.8 copy-start.1
  108.8 1.0 copy-start.2
  108.8 1.1 copy-start.3
  108.8 141.7 %all-reduce.8.cloned.1.call-start = ((), (), s32[]{:S(2)}) async-start(), calls=%async_computation.5 | async-start | bytes 262144 | tf_op jit(solution)/shard_map/psum | solution.py:51
  111.2 173.0 %all-reduce.6.cloned.1.call-start = ((), (), s32[]{:S(2)}) async-start(), calls=%async_computation.4 | async-start | bytes 524288 | tf_op jit(solution)/shard_map/psum | solution.py:48
Sparse Core Ops, SparseCore 0:
  10.1 51.7 all-gather.1
  68.1 30.8 all-reduce.3
  108.9 68.2 reduce-scatter.1
  181.0 69.4 all-reduce.7
  252.7 31.3 all-reduce.5
where the time goes:
time: 294 us
  waiting for transfers between devices  237 us (81%)
  blocking collectives  19.7 us (7%)
  between operations  14.6 us (5%)
  local copies, waits for them, and re-layouts  11.6 us (4%)
  matrix products  9.66 us (3%)
    reduce_scatter x1, waiting for transfers between devices, per_device(): lax.psum_scatter(lax.slice_in_dim(placed, 0, rows_here * lax.axis_size('l...  66 us
    psum x1, waiting for transfers between devices, per_device(): grad_weight, grad_bias = lax.psum((weight_term, bias_term), 'loop')  53.6 us
    all_gather x1, waiting for transfers between devices, per_device(): gathered = lax.all_gather(features, 'loop', axis=0, tiled=True)  52 us
    psum x1, waiting for transfers between devices, per_device(): own_rows = lax.psum(term, 'rep')  33.6 us
    psum x1, waiting for transfers between devices, per_device(): lax.psum(jnp.einsum('kb,kif->bif', row_pick, products, precision=highest)...  30.8 us
    psum x1, blocking collectives, per_device(): grad_weight, grad_bias = lax.psum((weight_term, bias_term), 'loop')  19.7 us
  transfers between devices with their start and end apart: 5, of which 5 were waited for; matrix products, arithmetic and copies ran while one was open for 1% of the time, Pallas kernels for 0%

commit v1 on v0

--- a/solution.py
+++ b/solution.py
@@ -45,7 +45,7 @@
         scatter_dimension=0,
         tiled=True,
     )
-    own_rows = lax.psum(term, "rep")
+    own_rows = jnp.sum(lax.all_gather(term, "rep"), axis=0)
     weight_term = jnp.dot(aggregated.T, gradient, precision=highest)
     bias_term = jnp.sum(gradient, axis=0)
     grad_weight, grad_bias = lax.psum((weight_term, bias_term), "loop")

time: 294 us -> 277 us (0.942)
  waiting for transfers between devices: 237 us -> 220 us
    psum x1 -> x0, waiting for transfers between devices: 33.6 us -> none  [per_device(): own_rows = lax.psum(term, 'rep')]
    psum x1, waiting for transfers between devices: 53.6 us -> 68.4 us  [per_device(): grad_weight, grad_bias = lax.psum((weight_term, bias_term), 'loop')]
  transfers between devices with their start and end apart: 5 -> 5, of which waited for: 5 -> 4; matrix products, arithmetic and copies ran while one was open for 1% -> 2% of each run, Pallas kernels for 0% -> 0%
where the time goes in v1:
time: 277 us
  waiting for transfers between devices  220 us (79%)
  blocking collectives  19.6 us (7%)
  between operations  14.6 us (5%)
  matrix products  9.67 us (3%)
  local copies, waits for them, and re-layouts  8.94 us (3%)
  other arithmetic  3.42 us (1%)
    reduce_scatter x1, waiting for transfers between devices, per_device(): lax.psum_scatter(lax.slice_in_dim(placed, 0, rows_here * lax.axis_size('l...  68.4 us
    psum x1, waiting for transfers between devices, per_device(): grad_weight, grad_bias = lax.psum((weight_term, bias_term), 'loop')  68.4 us
    all_gather x1, waiting for transfers between devices, per_device(): gathered = lax.all_gather(features, 'loop', axis=0, tiled=True)  52 us
    psum x1, waiting for transfers between devices, per_device(): lax.psum(jnp.einsum('kb,kif->bif', row_pick, products, precision=highest)...  30.8 us
    psum x1, blocking collectives, per_device(): grad_weight, grad_bias = lax.psum((weight_term, bias_term), 'loop')  19.6 us
  transfers between devices with their start and end apart: 5, of which 4 were waited for; matrix products, arithmetic and copies ran while one was open for 2% of the time, Pallas kernels for 0%

profile of v1, /device:TPU:0, one launch (start us, length us, event | category | flops | bytes accessed | tf_op | source)
XLA Modules:
  0.0 276.8 jit_solution(13177024379857865149)
XLA Ops:
  7.2 0.7 all-gather.4.cloned.1.call-update
  8.6 0.7 compare_select_fusion.1
  9.3 0.7 compare_select_fusion
  10.0 52.0 %all-gather.4.cloned.1.call-done = f32[4096,128]{1,0:T(8,128)} async-done(((f32[512,128]{1,0:T(8,128)}), f32[4096,128]{1,0:T(8,128)}) %all-gather.4.cloned.1.call-update) | async-done | bytes 2097168 | tf_op jit(solution)/shard_map/all_gather | solution.py:19
  62.0 2.2 gather_fusion
  64.2 1.8 fusion.16
  66.1 0.5 copy.14
  66.6 0.6 fusion.2
  67.2 0.7 copy.12
  68.1 30.8 %all-reduce.3.cloned.1.call-done = f32[512,128]{1,0:T(8,128)} async-done(((f32[512,128]{1,0:T(8,128)}), f32[512,128]{1,0:T(8,128)}) %all-reduce.3.cloned.1.call-update) | async-done | bytes 262160 | tf_op jit(solution)/shard_map/psum | solution.py:23
  98.9 2.5 fusion.15
  101.4 0.6 fusion.17
  102.0 0.2 copy-done.1
  102.2 0.6 gather_fusion.1
  102.8 1.8 fusion.18
  104.7 0.5 copy.15
  105.2 1.0 fusion
  106.2 2.6 copy.13
  108.9 68.4 %reduce-scatter.2.cloned.1.call-done = f32[512,128]{1,0:T(8,128)} async-done(((f32[4096,128]{1,0:T(8,128)}), f32[512,128]{1,0:T(8,128)}) %reduce-scatter.2.cloned.1.call-update) | async-done | bytes 262160 | tf_op jit(solution)/shard_map/reduce_scatter | solution.py:42
  177.3 1.3 fusion.19
  178.6 19.6 %psum.23 = f32[256]{0:T(256)} all-reduce(f32[256]{0:T(256)S(1)} %get-tuple-element.4), channel_id=1, replica_groups=mesh['loop'=8,'rep'=4] {'loop'}, use_global_device_ids=true, to_apply=%region_5.6 | all-reduce | flops 256 | bytes 2048 | tf_op jit(solution)/shard_map/psum | solution.py:51
  198.3 2.0 reduce_sum.18
  200.3 68.4 %all-reduce.5.cloned.1.call-done = f32[128,256]{1,0:T(8,128)} async-done(((f32[128,256]{1,0:T(8,128)}), f32[128,256]{1,0:T(8,128)}) %all-reduce.5.cloned.1.call-update) | async-done | bytes 131088 | tf_op jit(solution)/shard_map/psum | solution.py:51
  268.7 1.6 copy.19
  (29 shorter events, 0.4 us)
Async XLA Ops:
  7.2 57.0 %copy-start = (f32[16,128,128]{2,1,0:T(8,128)S(1)}, f32[16,128,128]{2,1,0:T(8,128)}, u32[]{:S(2)}) copy-start(f32[16,128,128]{2,1,0:T(8,128)} %param.11) | copy-start | bytes 3145732
  7.2 54.8 %all-gather.4.cloned.1.call-start = ((), (), s32[]{:S(2)}) async-start(), calls=%async_computation.1 | async-start | bytes 2359296 | tf_op jit(solution)/shard_map/all_gather | solution.py:19
  7.9 91.0 %all-reduce.3.cloned.1.call-start = ((), (), s32[]{:S(2)}) async-start(), calls=%async_computation.2 | async-start | bytes 524288 | tf_op jit(solution)/shard_map/psum | solution.py:23
  66.0 2.0 copy-start.5
  66.0 32.9 %copy-start.4 = (f32[128,256]{1,0:T(8,128)S(1)}, f32[128,256]{1,0:T(8,128)}, u32[]{:S(2)}) copy-start(f32[128,256]{1,0:T(8,128)} %param.9) | copy-start | bytes 393220
  66.0 32.9 %copy-start.7 = (f32[256]{0:T(256)S(1)}, f32[256]{0:T(256)}, u32[]{:S(2)}) copy-start(f32[256]{0:T(256)} %param.10) | copy-start | bytes 3076
  66.6 32.4 %copy-start.6 = (f32[512,256]{1,0:T(8,128)S(1)}, f32[512,256]{1,0:T(8,128)}, u32[]{:S(2)}) copy-start(f32[512,256]{1,0:T(8,128)} %param.15) | copy-start | bytes 1572868
  68.0 109.3 %reduce-scatter.2.cloned.1.call-start = ((), (), s32[]{:S(2)}) async-start(), calls=%async_computation.3 | async-start | bytes 2359296 | tf_op jit(solution)/shard_map/reduce_scatter | solution.py:42
  101.4 0.8 copy-start.1
  108.8 68.5 %copy-start.2 = (f32[512,256]{1,0:T(8,128)S(1)}, f32[512,256]{1,0:T(8,128)}, u32[]{:S(2)}) copy-start(f32[512,256]{1,0:T(8,128)} %copy-done.1) | copy-start | bytes 1572868
  108.8 68.5 %copy-start.3 = (f32[512,128]{1,0:T(8,128)S(1)}, f32[512,128]{1,0:T(8,128)}, u32[]{:S(2)}) copy-start(f32[512,128]{1,0:T(8,128)} %all-reduce.3.cloned.1.call-done) | copy-start | bytes 786436
  108.8 89.5 %all-gather.6.cloned.1.call-start = ((), (), s32[]{:S(2)}) async-start(), calls=%async_computation.5 | async-start | bytes 1310720 | tf_op jit(solution)/shard_map/all_gather | solution.py:48
  177.3 91.4 %all-reduce.5.cloned.1.call-start = ((), (), s32[]{:S(2)}) async-start(), calls=%async_computation.4 | async-start | bytes 262144 | tf_op jit(solution)/shard_map/psum | solution.py:51
Sparse Core Ops, SparseCore 0:
  10.1 51.7 all-gather.3
  68.1 30.8 all-reduce.2
  108.9 68.2 reduce-scatter.1
  178.7 15.6 all-gather.5
  198.2 70.4 all-reduce.4
